TPU v7x, 32 devices: a whole 2x2x4 slice. The times are simulated.
32 devices in a mesh: rep: 2 (over y), req: 4 (over z), mp: 4 (over x, core).
Axes of the slice: x: 2, y: 2, z: 4, core: 2. Of those that a mesh axis runs over, the one named last changes fastest.
Arguments:
- hidden_in: bfloat16 [128, 2, 8192], P(('rep', 'req'), None, 'mp'), parts along dimension 0, may hold values from -6 to 6
- frozen_query_rows: bfloat16 [128, 2, 8192], P(('rep', 'req'), None, 'mp'), parts along dimension 0, may hold values from -6 to 86
- new_kv: bfloat16 [128, 2, 2, 1024], P(('rep', 'req'), None, None, 'mp'), parts along dimension 0, may hold values from -6 to 31
- adapter_of: int32 [128], P(('rep', 'req')), parts along dimension 0, may hold values from 0 to 7, as said below
- adapter_home: int32 [16], P('rep'), parts along dimension 0, may hold values from 0 to 7, as said below
- a_store: bfloat16 [16, 64, 8192], P(('rep', 'req'), None, 'mp'), parts along dimension 0, may hold values from -0.0625 to 0.0625
- b_store: bfloat16 [16, 64, 8192], P(('rep', 'req'), None, 'mp'), parts along dimension 0, may hold values from -0.75 to 0.75
- kv_pool: bfloat16 [2, 1024, 16, 1024], P(None, ('rep', 'req'), None, 'mp'), parts along dimension 1, may hold values from -6 to 31
- page_table: int32 [128, 8], P(('rep', 'req')), parts along dimension 0, may hold values from 0 to 127, as said below
- cached_len: int32 [128], P(('rep', 'req')), parts along dimension 0, may hold values from 32 to 128
- new_group: int32 [128], P(('rep', 'req')), parts along dimension 0, may hold values from 0 to 3, as said below
Outputs:
- attended: bfloat16 [128, 2, 8192], P(('rep', 'req'), None, 'mp'), parts along dimension 0
- cache: bfloat16 [2, 128, 128, 1024], P(None, ('rep', 'req'), None, 'mp'), parts along dimension 1
There are 2 independent parts, one for each index of `rep`. A program takes and returns all parts, laid end to end along the dimension named above; each array names one. Nothing has to cross between parts.
Inputs may be any that keep to these rules, and one draw needn't show every extreme that they name: A permutation: adapter a lives in store slot adapter_home[a], which belongs to group adapter_home[a] div 2. `adapter_of`: the requests of one group (new rows h * 16 to h * 16 + 15) use adapters of min(16, number of groups) different owners, at most 4 requests an owner, a number reached in every group; all requests of one group whose adapters have one owner use the same adapter. `page_table`: the rows of one group name each of its 128 pages once. `new_group`: A request keeps its slot (row mod 16); the same 4 slots keep their group in every group; every group receives exactly one request into each slot; no group sends more than 3 requests to one other group, and some pair of groups reaches it.
All inputs are finite; a program needn't handle non-finite values.
Results may differ from a plain program's by a relative error of at most 0.0069.
Values may be sent and summed in bfloat16 or wider, within the bound.
A program may use at most 64 MiB of HBM per device.

v0:
```python
import jax
import jax.numpy as jnp
from jax import lax
from jax.sharding import PartitionSpec as P

HEAD = 128
NEG_FILL = -1e30


def attend(query_vectors, cached_keys, cached_values, length, fresh_kv):
    row_count, step_count, q_width = query_vectors.shape
    context = cached_keys.shape[1]
    kv_width = cached_keys.shape[2]
    kv_heads = kv_width // HEAD
    per_kv = q_width // kv_width
    score_scale = HEAD ** (-0.5)
    q_split = query_vectors.reshape(row_count, step_count, kv_heads, per_kv, HEAD)
    k_split = cached_keys.reshape(row_count, context, kv_heads, HEAD)
    v_split = cached_values.reshape(row_count, context, kv_heads, HEAD)
    new_keys = fresh_kv[:, :, 0].reshape(row_count, step_count, kv_heads, HEAD)
    new_values = fresh_kv[:, :, 1].reshape(row_count, step_count, kv_heads, HEAD)
    old_scores = (
        jnp.einsum("bskgd,bjkd->bskgj", q_split, k_split, preferred_element_type=jnp.float32)
        * score_scale
    )
    visible = jnp.arange(context)[None, :] < length[:, None]
    old_scores = jnp.where(visible[:, None, None, None, :], old_scores, NEG_FILL)
    new_scores = (
        jnp.einsum("bskgd,btkd->bskgt", q_split, new_keys, preferred_element_type=jnp.float32)
        * score_scale
    )
    causal = jnp.arange(step_count)[None, :] <= jnp.arange(step_count)[:, None]
    new_scores = jnp.where(causal[None, :, None, None, :], new_scores, NEG_FILL)
    scores = jnp.concatenate([old_scores, new_scores], axis=-1)
    row_max = jnp.max(scores, axis=-1, keepdims=True)
    weights = jnp.exp(scores - row_max)
    probabilities = (weights / jnp.sum(weights, axis=-1, keepdims=True)).astype(jnp.bfloat16)
    attention_out = jnp.einsum(
        "bskgj,bjkd->bskgd",
        probabilities[..., :context],
        v_split,
        preferred_element_type=jnp.float32,
    )
    attention_out = attention_out + jnp.einsum(
        "bskgt,btkd->bskgd",
        probabilities[..., context:],
        new_values,
        preferred_element_type=jnp.float32,
    )
    return attention_out.reshape(row_count, step_count, q_width).astype(jnp.bfloat16)


def adapter_rank_width(rank_partial_sum):
    return lax.psum(rank_partial_sum, "mp")


def per_device(
    hidden_in,
    frozen_query_rows,
    new_kv,
    adapter_of,
    adapter_home,
    a_store,
    b_store,
    kv_pool,
    page_table,
    cached_len,
    new_group,
):
    groups = lax.axis_size("req")
    my_group = lax.axis_index("req")
    per_group = adapter_of.shape[0]
    store_count = a_store.shape[0]
    context = page_table.shape[1] * kv_pool.shape[2]
    kv_width = kv_pool.shape[3]
    move_cap = -(-(per_group - per_group // 4) // groups)
    group_ids = jnp.arange(groups, dtype=jnp.int32)
    slot_ids = jnp.arange(per_group, dtype=jnp.int32)
    buffer_ids = jnp.arange(groups * move_cap, dtype=jnp.int32)
    adapter_slot = jnp.take(adapter_home, adapter_of)
    owners = adapter_slot // store_count
    local_pick = adapter_slot % store_count
    owner_hit = owners[:, None] == group_ids[None, :]
    wanted = jnp.max(jnp.where(owner_hit, local_pick[:, None], -1), axis=0)
    moving = new_group != my_group
    dest_hit = (new_group[:, None] == group_ids[None, :]) & moving[:, None]
    order_in = jnp.cumsum(dest_hit.astype(jnp.int32), axis=0) - 1
    position = jnp.sum(jnp.where(dest_hit, order_in, 0), axis=1)
    flat_slot = jnp.where(moving, new_group * move_cap + position, -1)
    slot_match = flat_slot[None, :] == buffer_ids[:, None]
    send_src = jnp.where(
        jnp.any(slot_match, axis=1),
        jnp.sum(jnp.where(slot_match, slot_ids[None, :], 0), axis=1),
        -1,
    )
    safe_src = jnp.maximum(send_src, 0)
    send_len = jnp.where(send_src >= 0, jnp.take(cached_len, safe_src), 0)
    got_wanted, got_slots, got_lens = (
        lax.all_to_all(wanted, "req", split_axis=0, concat_axis=0, tiled=True),
        lax.all_to_all(
            send_src.reshape(groups, move_cap), "req", split_axis=0, concat_axis=0, tiled=True
        ),
        lax.all_to_all(
            send_len.reshape(groups, move_cap), "req", split_axis=0, concat_axis=0, tiled=True
        ),
    )
    page_rows = jnp.take(kv_pool, page_table.reshape(-1), axis=1)
    cache_old = page_rows.reshape(2, per_group, context, kv_width)
    incoming = got_slots.reshape(-1)
    in_match = incoming[None, :] == slot_ids[:, None]
    in_index = jnp.sum(jnp.where(in_match, buffer_ids[None, :], 0), axis=1)
    len_new = jnp.where(moving, jnp.take(got_lens.reshape(-1), in_index), cached_len)
    wanted_slot = jnp.maximum(got_wanted, 0)
    a_panels, b_panels = (
        lax.all_to_all(
            jnp.take(a_store, wanted_slot, axis=0), "req", split_axis=0, concat_axis=0, tiled=True
        ),
        lax.all_to_all(
            jnp.take(b_store, wanted_slot, axis=0), "req", split_axis=0, concat_axis=0, tiled=True
        ),
    )
    a_rows = jnp.take(a_panels, owners, axis=0)
    up_panel_rows = jnp.take(b_panels, owners, axis=0)
    rank_slice_product = jnp.einsum(
        "rsd,rkd->rsk", hidden_in, a_rows, preferred_element_type=jnp.float32
    )
    complete_rank_product = adapter_rank_width(rank_slice_product).astype(jnp.bfloat16)
    adapter_query_delta = jnp.einsum(
        "gxj,gjv->gxv", complete_rank_product, up_panel_rows, preferred_element_type=jnp.float32
    )
    query_vectors = (frozen_query_rows.astype(jnp.float32) + adapter_query_delta).astype(
        jnp.bfloat16
    )
    far_cache = jnp.take(cache_old, safe_src, axis=1)
    send_pages = far_cache.reshape(2, groups, move_cap, context, kv_width)
    got_pages = lax.all_to_all(send_pages, "req", split_axis=1, concat_axis=1, tiled=True)
    pooled = jnp.concatenate(
        [cache_old, got_pages.reshape(2, groups * move_cap, context, kv_width)], axis=1
    )
    source = jnp.where(moving, per_group + in_index, slot_ids)
    cache_new = jnp.take(pooled, source, axis=1)
    attended = attend(query_vectors, cache_new[0], cache_new[1], len_new, new_kv)
    return (attended, cache_new)


def solution(mesh):
    placed = (
        P(("rep", "req"), None, "mp"),
        P(("rep", "req"), None, "mp"),
        P(("rep", "req"), None, None, "mp"),
        P(("rep", "req")),
        P("rep"),
        P(("rep", "req"), None, "mp"),
        P(("rep", "req"), None, "mp"),
        P(None, ("rep", "req"), None, "mp"),
        P(("rep", "req"), None),
        P(("rep", "req")),
        P(("rep", "req")),
    )
    return jax.shard_map(
        per_device,
        mesh=mesh,
        in_specs=placed,
        out_specs=(P(("rep", "req"), None, "mp"), P(None, ("rep", "req"), None, "mp")),
        check_vma=False,
    )
```

profile of v0, /device:TPU:0, one launch (start us, length us, event | category | flops | bytes accessed | tf_op | source)
XLA Modules:
  0.0 155.8 jit_solution(11224241576532435948)
XLA Ops:
  0.6 0.8 compare_select_fusion.3
  1.5 1.3 gather_fusion.5
  2.8 0.7 compare_and_fusion.1
  3.6 0.7 copy.112
  4.2 6.3 %all-to-all-start.3 = ((s32[4,1,1]{2,1,0:T(1,128)}), s32[4,1,1]{2,1,0:T(1,128)S(1)}, u32[]{:S(2)}, u32[]{:S(2)}) async-start(s32[4,1,1]{2,1,0:T(1,128)} %copy.112), calls=%async_computation.3 | async-start | bytes 4096 | tf_op jit(solution)/shard_map/all_to_all | solution.py:99
  10.5 0.7 broadcast_compare_fusion.1
  11.2 0.7 fusion.34
  12.0 0.8 select_reduce_fusion.3
  12.8 0.7 add_select_fusion
  13.5 0.1 fusion.32
  13.7 0.7 select_n.200
  14.4 1.3 gather_fusion.3
  15.8 1.3 select_select_fusion
  17.1 5.1 %all-to-all-start = ((s32[4,1,3]{2,1,0:T(1,128)}), s32[4,1,3]{2,1,0:T(1,128)S(1)}, u32[]{:S(2)}, u32[]{:S(2)}) async-start(s32[4,1,3]{2,1,0:T(1,128)} %bitcast), calls=%async_computation | async-start | bytes 4096 | tf_op jit(solution)/shard_map/all_to_all | solution.py:100
  22.2 0.2 maximum_reduce_fusion
  22.4 1.7 %gather_fusion.6 = bf16[4,64,2048]{2,1,0:T(8,128)(2,1)S(1)} fusion(bf16[2,64,2048]{2,1,0:T(8,128)(2,1)} %param.20, s32[1024]{0:T(1024)S(1)} %pad_clamp_fusion.1), kind=kCustom, calls=%fused_computation.clone | custom fusion | bytes 2097168 | tf_op jit(solution)/shard_map/jit(_take)/gather | solution.py:116
  24.0 2.6 %gather_fusion.8 = bf16[4,64,2048]{2,1,0:T(8,128)(2,1)} fusion(bf16[2,64,2048]{2,1,0:T(8,128)(2,1)} %param.21, s32[1024]{0:T(1024)S(1)} %pad_clamp_fusion.1), kind=kCustom, calls=%fused_computation.2.clone | custom fusion | bytes 2097168 | tf_op jit(solution)/shard_map/jit(_take)/gather | solution.py:119
  26.7 1.0 all-to-all-done
  27.6 4.1 %all-to-all-start.2 = ((s32[4,1,3]{2,1,0:T(1,128)}), s32[4,1,3]{2,1,0:T(1,128)S(1)}, u32[]{:S(2)}, u32[]{:S(2)}) async-start(s32[4,1,3]{2,1,0:T(1,128)} %bitcast.10), calls=%async_computation.2 | async-start | bytes 4096 | tf_op jit(solution)/shard_map/all_to_all | solution.py:103
  31.8 2.8 %broadcast_select_fusion.1 = (bf16[4,64,2048]{2,1,0:T(8,128)(2,1)}, bf16[4,64,2048]{2,1,0:T(8,128)(2,1)}) fusion(bf16[4,64,2048]{2,1,0:T(8,128)(2,1)S(1)} %gather_fusion.6, pred[4]{0:T(512)(128)(4,1)S(1)} %compare_and_fusion.2, bf16[4,64,2048]{2,1,0:T(8,128)(2,1)} %gather_fusion.8), kind=kLoop, calls=%fused_computation.36 | loop fusion | flops 1048576 | bytes 4194308 | tf_op jit(solution)/shard_map/jit(_take)/select_n | solution.py:116
  34.6 2.6 %all-to-all-done.2 = s32[4,1,3]{2,1,0:T(1,128)S(1)} async-done(((s32[4,1,3]{2,1,0:T(1,128)}), s32[4,1,3]{2,1,0:T(1,128)S(1)}, u32[]{:S(2)}, u32[]{:S(2)}) %all-to-all-start.2) | async-done | bytes 80 | tf_op jit(solution)/shard_map/all_to_all | solution.py:103
  37.1 3.5 %all-to-all-start.4 = ((bf16[4,64,2048]{2,1,0:T(8,128)(2,1)}), bf16[4,64,2048]{2,1,0:T(8,128)(2,1)S(1)}, u32[]{:S(2)}, u32[]{:S(2)}) async-start(bf16[4,64,2048]{2,1,0:T(8,128)(2,1)} %get-tuple-element.25), calls=%async_computation.4 | async-start | bytes 2097152 | tf_op jit(solution)/shard_map/all_to_all | solution.py:115
  40.8 23.4 %all-to-all-done.4 = bf16[4,64,2048]{2,1,0:T(8,128)(2,1)S(1)} async-done(((bf16[4,64,2048]{2,1,0:T(8,128)(2,1)}), bf16[4,64,2048]{2,1,0:T(8,128)(2,1)S(1)}, u32[]{:S(2)}, u32[]{:S(2)}) %all-to-all-start.4) | async-done | bytes 1048608 | tf_op jit(solution)/shard_map/all_to_all | solution.py:115
  64.2 4.2 %all-to-all-start.5 = ((bf16[4,64,2048]{2,1,0:T(8,128)(2,1)}), bf16[4,64,2048]{2,1,0:T(8,128)(2,1)}, u32[]{:S(2)}, u32[]{:S(2)}) async-start(bf16[4,64,2048]{2,1,0:T(8,128)(2,1)} %get-tuple-element.26), calls=%async_computation.5 | async-start | bytes 2097152 | tf_op jit(solution)/shard_map/all_to_all | solution.py:118
  68.5 2.0 %gather_fusion = bf16[128,2,16,256]{3,2,1,0:T(8,128)(2,1)} fusion(bf16[2,128,16,256]{3,2,1,0:T(8,128)(2,1)S(1)} %copy-done, s32[1024]{0:T(1024)S(1)} %pad_clamp_fusion.6), kind=kCustom, calls=%fused_computation.4 | custom fusion | bytes 4194816 | tf_op jit(solution)/shard_map/jit(_take)/gather | solution.py:107
  70.5 3.1 %copy.106 = bf16[2,128,16,256]{3,2,1,0:T(8,128)(2,1)} copy(bf16[2,128,16,256]{3,2,0,1:T(8,128)(2,1)} %bitcast.52) | data formatting | bytes 4194304 | tf_op jit(solution)/shard_map/jit(_take)/gather | solution.py:107
  73.9 2.8 %bitcast_select_fusion = bf16[2,16,128,256]{3,2,1,0:T(8,128)(2,1)} fusion(pred[16,128]{1,0:T(8,128)(4,1)S(1)} %broadcast_in_dim.159, bf16[2,16,128,256]{3,2,1,0:T(8,128)(2,1)} %bitcast.51), kind=kLoop, calls=%fused_computation.19 | loop fusion | flops 1048576 | bytes 4196352 | tf_op jit(solution)/shard_map/jit(_take)/select_n | solution.py:107
  76.7 3.4 %gather_fusion.1 = bf16[12,2,128,256]{3,2,1,0:T(8,128)(2,1)} fusion(bf16[2,16,128,256]{3,2,1,0:T(8,128)(2,1)} %bitcast_select_fusion, s32[1024]{0:T(1024)S(1)} %pad_clamp_fusion.5), kind=kCustom, calls=%fused_computation.5 | custom fusion | bytes 3145776 | tf_op jit(solution)/shard_map/jit(_take)/gather | solution.py:134
  80.2 0.2 slice_reduce_fusion
  80.4 0.6 reshape.370
  81.0 2.9 %copy_select_fusion = bf16[2,4,3,128,256]{4,3,2,0,1:T(8,128)(2,1)} fusion(bf16[2,4,3,128,256]{4,3,0,2,1:T(8,128)(2,1)} %bitcast.54, pred[4,3]{1,0:T(4,128)(4,1)S(1)} %le.81), kind=kLoop, calls=%fused_computation.23 | loop fusion | flops 786432 | bytes 3145740 | tf_op jit(solution)/shard_map/jit(_take)/select_n | solution.py:134
  83.9 9.9 %all-to-all-done.5 = bf16[4,64,2048]{2,1,0:T(8,128)(2,1)} async-done(((bf16[4,64,2048]{2,1,0:T(8,128)(2,1)}), bf16[4,64,2048]{2,1,0:T(8,128)(2,1)}, u32[]{:S(2)}, u32[]{:S(2)}) %all-to-all-start.5) | async-done | bytes 1048608 | tf_op jit(solution)/shard_map/all_to_all | solution.py:118
  93.8 4.3 %all-to-all-start.1 = ((bf16[2,4,3,128,256]{4,3,2,0,1:T(8,128)(2,1)}), bf16[2,4,3,128,256]{4,3,2,0,1:T(8,128)(2,1)}, u32[]{:S(2)}, u32[]{:S(2)}) async-start(bf16[2,4,3,128,256]{4,3,2,0,1:T(8,128)(2,1)} %copy_select_fusion), calls=%async_computation.1 | async-start | bytes 3145728 | tf_op jit(solution)/shard_map/all_to_all | solution.py:136
  98.1 0.6 iota_compare_fusion.5
  98.7 0.5 broadcast.414
  99.3 0.6 reduce.14
  100.0 0.6 reduce.15
  100.8 0.7 gather_fusion.4
  101.5 0.6 compare_and_fusion.3
  102.1 0.6 pad_clamp_fusion.4
  102.7 0.7 iota_compare_fusion.1
  103.3 2.8 %gather_fusion.7 = bf16[16,64,2048]{2,1,0:T(8,128)(2,1)} fusion(bf16[4,64,2048]{2,1,0:T(8,128)(2,1)S(1)} %all-to-all-done.4, s32[1024]{0:T(1024)S(1)} %pad_clamp_fusion), kind=kCustom, calls=%fused_computation.1.clone | custom fusion | bytes 8388672 | tf_op jit(solution)/shard_map/jit(_take)/gather | solution.py:122
  106.1 4.0 %gather_fusion.9 = bf16[16,64,2048]{2,1,0:T(8,128)(2,1)} fusion(bf16[4,64,2048]{2,1,0:T(8,128)(2,1)} %all-to-all-done.5, s32[1024]{0:T(1024)S(1)} %pad_clamp_fusion), kind=kCustom, calls=%fused_computation.3.clone | custom fusion | bytes 8388672 | tf_op jit(solution)/shard_map/jit(_take)/gather | solution.py:123
  110.1 3.5 %fusion.20 = f32[16,2,64]{2,1,0:T(2,128)S(1)} fusion(bf16[16,2,2048]{2,1,0:T(2,128)(2,1)S(1)} %copy-done.9, bf16[16,64,2048]{2,1,0:T(8,128)(2,1)} %gather_fusion.7, pred[16]{0:T(512)(128)(4,1)S(1)} %get-tuple-element.16), kind=kOutput, calls=%fused_computation.34 | convolution fusion | flops 10485760 | bytes 4333584 | tf_op jit(solution)/shard_map/rsd,rkd->rsk/dot_general | solution.py:124
  113.6 10.2 %psum.7 = bf16[16,2,64]{2,1,0:T(2,128)(2,1)S(1)} all-reduce(f32[16,2,64]{2,1,0:T(2,128)S(1)} %fusion.20), channel_id=1, replica_groups=mesh['rep'=2,'req'=4,'mp'=4] {'mp'}, use_global_device_ids=true, to_apply=%region_6.9 | all-reduce | flops 2048 | bytes 12288 | tf_op jit(solution)/shard_map/psum | solution.py:54
  123.8 2.9 %fusion.9 = bf16[16,2,2048]{2,1,0:T(2,128)(2,1)S(1)} fusion(bf16[16,64,2048]{2,1,0:T(8,128)(2,1)} %gather_fusion.9, pred[16]{0:T(512)(128)(4,1)S(1)} %get-tuple-element.16, bf16[16,2,2048]{2,1,0:T(2,128)(2,1)S(1)} %copy-done.10, bf16[16,2,64]{2,1,0:T(2,128)(2,1)S(1)} %psum.7), kind=kOutput, calls=%fused_computation.18 | convolution fusion | flops 10682368 | bytes 4460560 | tf_op jit(solution)/shard_map/gxj,gjv->gxv/dot_general | solution.py:128
  126.9 0.9 fusion.42
  127.8 6.8 %all-to-all-done.1 = bf16[2,4,3,128,256]{4,3,2,0,1:T(8,128)(2,1)} async-done(((bf16[2,4,3,128,256]{4,3,2,0,1:T(8,128)(2,1)}), bf16[2,4,3,128,256]{4,3,2,0,1:T(8,128)(2,1)}, u32[]{:S(2)}, u32[]{:S(2)}) %all-to-all-start.1) | async-done | bytes 1572896 | tf_op jit(solution)/shard_map/all_to_all | solution.py:136
  134.6 1.7 %copy.108 = bf16[2,4,3,128,256]{4,3,2,1,0:T(8,128)(2,1)S(1)} copy(bf16[2,4,3,128,256]{4,3,2,0,1:T(8,128)(2,1)} %all-to-all-done.1) | data formatting | bytes 3145728 | tf_op jit(solution)/shard_map/all_to_all | solution.py:136
  136.3 0.4 copy-done.2
  136.7 2.1 %pad_maximum_fusion = bf16[2,28,128,256]{3,2,1,0:T(8,128)(2,1)} fusion(bf16[2,12,128,256]{3,2,1,0:T(8,128)(2,1)S(1)} %bitcast.53, bf16[2,16,128,256]{3,2,1,0:T(8,128)(2,1)S(1)} %copy-done.2), kind=kLoop, calls=%fused_computation.16 | loop fusion | flops 1835008 | bytes 7340032 | tf_op jit(solution)/shard_map/concatenate | solution.py:137
  138.8 4.2 %gather_fusion.2 = bf16[16,2,128,256]{3,2,1,0:T(8,128)(2,1)} fusion(bf16[2,28,128,256]{3,2,1,0:T(8,128)(2,1)} %pad_maximum_fusion, s32[1024]{0:T(1024)} %pad_clamp_fusion.4), kind=kCustom, calls=%fused_computation.6 | custom fusion | bytes 4194368 | tf_op jit(solution)/shard_map/jit(_take)/gather | solution.py:141
  143.0 1.9 %select_bitcast_fusion = bf16[2,16,128,256]{3,2,0,1:T(8,128)(2,1)S(1)} fusion(bf16[16,2,128,256]{3,2,1,0:T(8,128)(2,1)} %gather_fusion.2, pred[16]{0:T(512)(128)(4,1)S(1)} %copy-done.8), kind=kLoop, calls=%fused_computation.22 | loop fusion | flops 1048576 | bytes 4194320 | tf_op jit(solution)/shard_map/jit(_take)/select_n | solution.py:141
  144.8 1.5 fusion.40
  146.3 1.5 copy.125
  147.8 1.6 %copy.111 = bf16[1,16,128,256]{2,3,1,0:T(8,128)(2,1)S(1)} copy(bf16[1,16,128,256]{3,2,0,1:T(8,128)(2,1)} %get-tuple-element.23) | data formatting | bytes 2097152 | tf_op jit(solution)/shard_map/slice | solution.py:142
  149.4 1.2 fusion.41
  150.6 0.8 reduce_max.32
  151.4 0.3 fusion.24
  151.7 0.9 divide_convert_fusion
  152.6 1.7 %copy.109 = bf16[1,16,128,256]{2,3,1,0:T(8,128)(2,1)S(1)} copy(bf16[1,16,128,256]{3,2,0,1:T(8,128)(2,1)} %get-tuple-element.24) | data formatting | bytes 2097152 | tf_op jit(solution)/shard_map/slice | solution.py:142
  154.3 0.6 convolution_bitcast_fusion.1
  154.9 0.2 fusion.19
  155.1 0.7 reshape.372
  (56 shorter events, 1.4 us)
Async XLA Ops:
  0.6 67.9 %copy-start = (bf16[2,128,16,256]{3,2,1,0:T(8,128)(2,1)S(1)}, bf16[2,128,16,256]{3,2,1,0:T(8,128)(2,1)}, u32[]{:S(2)}) copy-start(bf16[2,128,16,256]{3,2,1,0:T(8,128)(2,1)} %param.22) | copy-start | bytes 6291460
  4.2 12.9 %all-to-all-start.3 = ((s32[4,1,1]{2,1,0:T(1,128)}), s32[4,1,1]{2,1,0:T(1,128)S(1)}, u32[]{:S(2)}, u32[]{:S(2)}) async-start(s32[4,1,1]{2,1,0:T(1,128)} %copy.112), calls=%async_computation.3 | async-start | bytes 4096 | tf_op jit(solution)/shard_map/all_to_all | solution.py:99
  17.1 10.6 %all-to-all-start = ((s32[4,1,3]{2,1,0:T(1,128)}), s32[4,1,3]{2,1,0:T(1,128)S(1)}, u32[]{:S(2)}, u32[]{:S(2)}) async-start(s32[4,1,3]{2,1,0:T(1,128)} %bitcast), calls=%async_computation | async-start | bytes 4096 | tf_op jit(solution)/shard_map/all_to_all | solution.py:100
  27.6 9.5 %all-to-all-start.2 = ((s32[4,1,3]{2,1,0:T(1,128)}), s32[4,1,3]{2,1,0:T(1,128)S(1)}, u32[]{:S(2)}, u32[]{:S(2)}) async-start(s32[4,1,3]{2,1,0:T(1,128)} %bitcast.10), calls=%async_computation.2 | async-start | bytes 4096 | tf_op jit(solution)/shard_map/all_to_all | solution.py:103
  34.6 6.1 %copy-start.5 = (s32[16,8]{0,1:T(8,128)S(1)}, s32[16,8]{0,1:T(8,128)}, u32[]{:S(2)}) copy-start(s32[16,8]{0,1:T(8,128)} %param.23) | copy-start | bytes 1540
  37.1 27.1 %all-to-all-start.4 = ((bf16[4,64,2048]{2,1,0:T(8,128)(2,1)}), bf16[4,64,2048]{2,1,0:T(8,128)(2,1)S(1)}, u32[]{:S(2)}, u32[]{:S(2)}) async-start(bf16[4,64,2048]{2,1,0:T(8,128)(2,1)} %get-tuple-element.25), calls=%async_computation.4 | async-start | bytes 2097152 | tf_op jit(solution)/shard_map/all_to_all | solution.py:115
  64.2 29.5 %all-to-all-start.5 = ((bf16[4,64,2048]{2,1,0:T(8,128)(2,1)}), bf16[4,64,2048]{2,1,0:T(8,128)(2,1)}, u32[]{:S(2)}, u32[]{:S(2)}) async-start(bf16[4,64,2048]{2,1,0:T(8,128)(2,1)} %get-tuple-element.26), calls=%async_computation.5 | async-start | bytes 2097152 | tf_op jit(solution)/shard_map/all_to_all | solution.py:118
  76.7 3.5 %copy-start.4 = (bf16[16,2,2,256]{3,2,1,0:T(2,128)(2,1)S(1)}, bf16[16,2,2,256]{3,2,1,0:T(2,128)(2,1)}, u32[]{:S(2)}) copy-start(bf16[16,2,2,256]{3,2,1,0:T(2,128)(2,1)} %param.17) | copy-start | bytes 98308
  83.9 17.6 %copy-start.7 = (s32[16]{0:T(128)S(1)}, s32[16]{0:T(128)}, u32[]{:S(2)}) copy-start(s32[16]{0:T(128)} %param.25) | copy-start | bytes 196
  83.9 18.8 %copy-start.1 = (s32[16]{0:T(128)S(1)}, s32[16]{0:T(128)}, u32[]{:S(2)}) copy-start(s32[16]{0:T(128)} %param.24) | copy-start | bytes 196
  93.8 40.9 %all-to-all-start.1 = ((bf16[2,4,3,128,256]{4,3,2,0,1:T(8,128)(2,1)}), bf16[2,4,3,128,256]{4,3,2,0,1:T(8,128)(2,1)}, u32[]{:S(2)}, u32[]{:S(2)}) async-start(bf16[2,4,3,128,256]{4,3,2,0,1:T(8,128)(2,1)} %copy_select_fusion), calls=%async_computation.1 | async-start | bytes 3145728 | tf_op jit(solution)/shard_map/all_to_all | solution.py:136
  106.1 4.0 %copy-start.9 = (bf16[16,2,2048]{2,1,0:T(2,128)(2,1)S(1)}, bf16[16,2,2048]{2,1,0:T(2,128)(2,1)}, u32[]{:S(2)}) copy-start(bf16[16,2,2048]{2,1,0:T(2,128)(2,1)} %param.15) | copy-start | bytes 393220
  110.1 13.7 %copy-start.10 = (bf16[16,2,2048]{2,1,0:T(2,128)(2,1)S(1)}, bf16[16,2,2048]{2,1,0:T(2,128)(2,1)}, u32[]{:S(2)}) copy-start(bf16[16,2,2048]{2,1,0:T(2,128)(2,1)} %param.16) | copy-start | bytes 393220
  123.8 3.1 %copy-start.6 = (bf16[16,2,2,128]{3,2,1,0:T(2,128)(2,1)S(1)}, bf16[16,2,2,128]{3,2,1,0:T(2,128)(2,1)}, u32[]{:S(2)}) copy-start(bf16[16,2,2,128]{3,2,1,0:T(2,128)(2,1)} %reshape.370) | copy-start | bytes 49156
  123.8 3.1 %copy-start.11 = (pred[2,2]{1,0:T(4,128)(4,1)S(1)}, pred[2,2]{1,0:T(4,128)(4,1)}, u32[]{:S(2)}) copy-start(pred[2,2]{1,0:T(4,128)(4,1)} %iota_compare_fusion.5) | copy-start | bytes 16
  134.6 2.1 %copy-start.2 = (bf16[2,16,128,256]{3,2,1,0:T(8,128)(2,1)S(1)}, bf16[2,16,128,256]{3,2,1,0:T(8,128)(2,1)}, u32[]{:S(2)}) copy-start(bf16[2,16,128,256]{3,2,1,0:T(8,128)(2,1)} %bitcast_select_fusion) | copy-start | bytes 6291460
  138.8 4.2 %copy-start.8 = (pred[16]{0:T(512)(128)(4,1)S(1)}, pred[16]{0:T(512)(128)(4,1)}, u32[]{:S(2)}) copy-start(pred[16]{0:T(512)(128)(4,1)} %get-tuple-element.19) | copy-start | bytes 52
  152.6 1.7 %copy-start.3 = (bf16[16,2,2,8,130]{4,3,1,2,0:T(8,128)(2,1)S(1)}, bf16[16,2,2,8,130]{4,3,1,2,0:T(8,128)(2,1)}, u32[]{:S(2)}) copy-start(bf16[16,2,2,8,130]{4,3,1,2,0:T(8,128)(2,1)} %divide_convert_fusion) | copy-start | bytes 399364
where the time goes:
time: 157 us; the launch traced here: 156 us
  waiting for transfers between devices  43.7 us (28%)
  local copies, waits for them, and re-layouts  39.6 us (25%)
  starting transfers between devices  27.6 us (18%)
  other arithmetic  24.5 us (16%)
  blocking collectives  10.2 us (6%)
  matrix products  9.32 us (6%)
    all_to_all x1, waiting for transfers between devices, per_device(): lax.all_to_all(jnp.take(a_store, wanted_slot, axis=0), 'req', split_axis=...  23.4 us
    psum x1, blocking collectives, adapter_rank_width(): return lax.psum(rank_partial_sum, 'mp')  10.2 us
    all_to_all x1, waiting for transfers between devices, per_device(): lax.all_to_all(jnp.take(b_store, wanted_slot, axis=0), 'req', split_axis=...  9.87 us
    all_to_all x1, waiting for transfers between devices, per_device(): lax.all_to_all(send_pages, 'req', split_axis=1, concat_axis=1, tiled=True)  6.84 us
    all_to_all x1, starting transfers between devices, per_device(): lax.all_to_all(wanted, 'req', split_axis=0, concat_axis=0, tiled=True)  6.32 us
    gather x2, local copies, waits for them, and re-layouts, per_device(): page_rows = jnp.take(kv_pool, page_table.reshape(-1), axis=1)  5.1 us
    all_to_all x1, starting transfers between devices, per_device(): lax.all_to_all(send_src.reshape(groups, move_cap), 'req', split_axis=0, c...  5.09 us
    all_to_all x1, starting transfers between devices, per_device(): lax.all_to_all(send_pages, 'req', split_axis=1, concat_axis=1, tiled=True)  4.35 us
  transfers between devices with their start and end apart: 6, of which 5 were waited for; matrix products, arithmetic and copies ran while one was open for 31% of the time, Pallas kernels for 0%

commit v1 on v0

--- a/solution.py
+++ b/solution.py
@@ -133,7 +133,10 @@
     )
     far_cache = jnp.take(cache_old, safe_src, axis=1)
     send_pages = far_cache.reshape(2, groups, move_cap, context, kv_width)
-    got_pages = lax.all_to_all(send_pages, "req", split_axis=1, concat_axis=1, tiled=True)
+    got_pages = jnp.concatenate(
+        lax.all_to_all(jnp.stack(jnp.split(send_pages, lax.axis_size("req"), axis=1)), "req", 0, 0),
+        axis=1,
+    )
     pooled = jnp.concatenate(
         [cache_old, got_pages.reshape(2, groups * move_cap, context, kv_width)], axis=1
     )

time: 157 us -> 157 us (level)
    all_to_all x1 -> x0, local copies, waits for them, and re-layouts: 1.7 us -> none  [per_device(): lax.all_to_all(send_pages, 'req', split_axis=1, concat_axis=1, tiled=True)]
    reshape x0 -> x1, local copies, waits for them, and re-layouts: none -> 1.7 us  [per_device(): jnp.concatenate(lax.all_to_all(jnp.stack(jnp.split(send_pages, lax.axis_s...]
where the time goes in v1:
time: 157 us; the launch traced here: 156 us
  waiting for transfers between devices  43.3 us (28%)
  local copies, waits for them, and re-layouts  39.8 us (25%)
  starting transfers between devices  27.6 us (18%)
  other arithmetic  24.7 us (16%)
  blocking collectives  10.2 us (6%)
  matrix products  9.32 us (6%)
    all_to_all x1, waiting for transfers between devices, per_device(): lax.all_to_all(jnp.take(a_store, wanted_slot, axis=0), 'req', split_axis=...  23.4 us
    psum x1, blocking collectives, adapter_rank_width(): return lax.psum(rank_partial_sum, 'mp')  10.2 us
    all_to_all x1, waiting for transfers between devices, per_device(): lax.all_to_all(jnp.take(b_store, wanted_slot, axis=0), 'req', split_axis=...  9.53 us
    all_to_all x1, waiting for transfers between devices, per_device(): lax.all_to_all(jnp.stack(jnp.split(send_pages, lax.axis_size('req'), axis...  6.84 us
    all_to_all x1, starting transfers between devices, per_device(): lax.all_to_all(wanted, 'req', split_axis=0, concat_axis=0, tiled=True)  6.32 us
    gather x2, local copies, waits for them, and re-layouts, per_device(): page_rows = jnp.take(kv_pool, page_table.reshape(-1), axis=1)  5.1 us
    all_to_all x1, starting transfers between devices, per_device(): lax.all_to_all(send_src.reshape(groups, move_cap), 'req', split_axis=0, c...  5.09 us
    all_to_all x1, starting transfers between devices, per_device(): lax.all_to_all(jnp.stack(jnp.split(send_pages, lax.axis_size('req'), axis...  4.35 us
  transfers between devices with their start and end apart: 6, of which 5 were waited for; matrix products, arithmetic and copies ran while one was open for 31% of the time, Pallas kernels for 0%

profile of v1, /device:TPU:0, one launch (start us, length us, event | category | flops | bytes accessed | tf_op | source)
XLA Modules:
  0.0 155.8 jit_solution(8466525121671804952)
XLA Ops:
  0.6 0.8 compare_select_fusion.3
  1.5 1.3 gather_fusion.5
  2.8 0.7 compare_and_fusion.1
  3.6 0.7 copy.121
  4.2 6.3 %all-to-all-start.3 = ((s32[4,1,1]{2,1,0:T(1,128)}), s32[4,1,1]{2,1,0:T(1,128)S(1)}, u32[]{:S(2)}, u32[]{:S(2)}) async-start(s32[4,1,1]{2,1,0:T(1,128)} %copy.121), calls=%async_computation.3 | async-start | bytes 4096 | tf_op jit(solution)/shard_map/all_to_all | solution.py:99
  10.5 0.7 broadcast_compare_fusion.1
  11.2 0.7 fusion.34
  12.0 0.8 select_reduce_fusion.3
  12.8 0.7 add_select_fusion
  13.7 0.7 select_n.200
  14.4 1.3 gather_fusion.3
  15.8 1.3 select_select_fusion
  17.1 5.1 %all-to-all-start = ((s32[4,1,3]{2,1,0:T(1,128)}), s32[4,1,3]{2,1,0:T(1,128)S(1)}, u32[]{:S(2)}, u32[]{:S(2)}) async-start(s32[4,1,3]{2,1,0:T(1,128)} %bitcast), calls=%async_computation | async-start | bytes 4096 | tf_op jit(solution)/shard_map/all_to_all | solution.py:100
  22.2 0.2 maximum_reduce_fusion
  22.4 1.7 %gather_fusion.6 = bf16[4,64,2048]{2,1,0:T(8,128)(2,1)S(1)} fusion(bf16[2,64,2048]{2,1,0:T(8,128)(2,1)} %param.20, s32[1024]{0:T(1024)S(1)} %pad_clamp_fusion.1), kind=kCustom, calls=%fused_computation.clone | custom fusion | bytes 2097168 | tf_op jit(solution)/shard_map/jit(_take)/gather | solution.py:116
  24.0 2.6 %gather_fusion.8 = bf16[4,64,2048]{2,1,0:T(8,128)(2,1)} fusion(bf16[2,64,2048]{2,1,0:T(8,128)(2,1)} %param.21, s32[1024]{0:T(1024)S(1)} %pad_clamp_fusion.1), kind=kCustom, calls=%fused_computation.2.clone | custom fusion | bytes 2097168 | tf_op jit(solution)/shard_map/jit(_take)/gather | solution.py:119
  26.7 1.0 all-to-all-done
  27.6 4.1 %all-to-all-start.2 = ((s32[4,1,3]{2,1,0:T(1,128)}), s32[4,1,3]{2,1,0:T(1,128)S(1)}, u32[]{:S(2)}, u32[]{:S(2)}) async-start(s32[4,1,3]{2,1,0:T(1,128)} %bitcast.15), calls=%async_computation.2 | async-start | bytes 4096 | tf_op jit(solution)/shard_map/all_to_all | solution.py:103
  31.8 2.8 %broadcast_select_fusion.1 = (bf16[4,64,2048]{2,1,0:T(8,128)(2,1)}, bf16[4,64,2048]{2,1,0:T(8,128)(2,1)}) fusion(bf16[4,64,2048]{2,1,0:T(8,128)(2,1)S(1)} %gather_fusion.6, pred[4]{0:T(512)(128)(4,1)S(1)} %compare_and_fusion.2, bf16[4,64,2048]{2,1,0:T(8,128)(2,1)} %gather_fusion.8), kind=kLoop, calls=%fused_computation.37 | loop fusion | flops 1048576 | bytes 4194308 | tf_op jit(solution)/shard_map/jit(_take)/select_n | solution.py:116
  34.6 2.6 %all-to-all-done.2 = s32[4,1,3]{2,1,0:T(1,128)S(1)} async-done(((s32[4,1,3]{2,1,0:T(1,128)}), s32[4,1,3]{2,1,0:T(1,128)S(1)}, u32[]{:S(2)}, u32[]{:S(2)}) %all-to-all-start.2) | async-done | bytes 80 | tf_op jit(solution)/shard_map/all_to_all | solution.py:103
  37.1 3.5 %all-to-all-start.4 = ((bf16[4,64,2048]{2,1,0:T(8,128)(2,1)}), bf16[4,64,2048]{2,1,0:T(8,128)(2,1)S(1)}, u32[]{:S(2)}, u32[]{:S(2)}) async-start(bf16[4,64,2048]{2,1,0:T(8,128)(2,1)} %get-tuple-element.29), calls=%async_computation.4 | async-start | bytes 2097152 | tf_op jit(solution)/shard_map/all_to_all | solution.py:115
  40.9 23.4 %all-to-all-done.4 = bf16[4,64,2048]{2,1,0:T(8,128)(2,1)S(1)} async-done(((bf16[4,64,2048]{2,1,0:T(8,128)(2,1)}), bf16[4,64,2048]{2,1,0:T(8,128)(2,1)S(1)}, u32[]{:S(2)}, u32[]{:S(2)}) %all-to-all-start.4) | async-done | bytes 1048608 | tf_op jit(solution)/shard_map/all_to_all | solution.py:115
  64.2 4.2 %all-to-all-start.5 = ((bf16[4,64,2048]{2,1,0:T(8,128)(2,1)}), bf16[4,64,2048]{2,1,0:T(8,128)(2,1)}, u32[]{:S(2)}, u32[]{:S(2)}) async-start(bf16[4,64,2048]{2,1,0:T(8,128)(2,1)} %get-tuple-element.30), calls=%async_computation.5 | async-start | bytes 2097152 | tf_op jit(solution)/shard_map/all_to_all | solution.py:118
  68.5 2.0 %gather_fusion = bf16[128,2,16,256]{3,2,1,0:T(8,128)(2,1)} fusion(bf16[2,128,16,256]{3,2,1,0:T(8,128)(2,1)S(1)} %copy-done, s32[1024]{0:T(1024)S(1)} %pad_clamp_fusion.6), kind=kCustom, calls=%fused_computation.4 | custom fusion | bytes 4194816 | tf_op jit(solution)/shard_map/jit(_take)/gather | solution.py:107
  70.5 3.1 %copy.115 = bf16[2,128,16,256]{3,2,1,0:T(8,128)(2,1)} copy(bf16[2,128,16,256]{3,2,0,1:T(8,128)(2,1)} %bitcast.61) | data formatting | bytes 4194304 | tf_op jit(solution)/shard_map/jit(_take)/gather | solution.py:107
  73.9 2.8 %bitcast_select_fusion = bf16[2,16,128,256]{3,2,1,0:T(8,128)(2,1)} fusion(pred[16,128]{1,0:T(8,128)(4,1)S(1)} %broadcast_in_dim.159, bf16[2,16,128,256]{3,2,1,0:T(8,128)(2,1)} %bitcast.60), kind=kLoop, calls=%fused_computation.19 | loop fusion | flops 1048576 | bytes 4196352 | tf_op jit(solution)/shard_map/jit(_take)/select_n | solution.py:107
  76.7 3.4 %gather_fusion.1 = bf16[12,2,128,256]{3,2,1,0:T(8,128)(2,1)} fusion(bf16[2,16,128,256]{3,2,1,0:T(8,128)(2,1)} %bitcast_select_fusion, s32[1024]{0:T(1024)S(1)} %pad_clamp_fusion.5), kind=kCustom, calls=%fused_computation.5 | custom fusion | bytes 3145776 | tf_op jit(solution)/shard_map/jit(_take)/gather | solution.py:134
  80.2 0.2 slice_reduce_fusion
  80.4 0.6 reshape.370
  81.0 1.6 %copy_select_fusion = bf16[2,4,3,128,256]{4,3,2,0,1:T(8,128)(2,1)S(1)} fusion(bf16[2,4,3,128,256]{4,3,0,2,1:T(8,128)(2,1)} %bitcast.63, pred[4,3]{1,0:T(4,128)(4,1)S(1)} %le.81), kind=kLoop, calls=%fused_computation.24 | loop fusion | flops 786432 | bytes 3145740 | tf_op jit(solution)/shard_map/jit(_take)/select_n | solution.py:134
  82.8 1.4 pad_maximum_fusion.1
  84.2 9.5 %all-to-all-done.5 = bf16[4,64,2048]{2,1,0:T(8,128)(2,1)} async-done(((bf16[4,64,2048]{2,1,0:T(8,128)(2,1)}), bf16[4,64,2048]{2,1,0:T(8,128)(2,1)}, u32[]{:S(2)}, u32[]{:S(2)}) %all-to-all-start.5) | async-done | bytes 1048608 | tf_op jit(solution)/shard_map/all_to_all | solution.py:118
  93.8 4.3 %all-to-all-start.1 = ((bf16[4,2,1,3,128,256]{5,4,3,1,2,0:T(8,128)(2,1)}), bf16[4,2,1,3,128,256]{5,4,3,1,2,0:T(8,128)(2,1)}, u32[]{:S(2)}, u32[]{:S(2)}) async-start(bf16[4,2,1,3,128,256]{5,4,3,1,2,0:T(8,128)(2,1)} %pad_maximum_fusion.1), calls=%async_computation.1 | async-start | bytes 3145728 | tf_op jit(solution)/shard_map/all_to_all | solution.py:137
  98.1 0.6 iota_compare_fusion.5
  98.7 0.5 broadcast.414
  99.3 0.6 reduce.14
  100.0 0.6 reduce.15
  100.8 0.7 gather_fusion.4
  101.5 0.6 compare_and_fusion.3
  102.1 0.6 pad_clamp_fusion.4
  102.7 0.7 iota_compare_fusion.1
  103.3 2.8 %gather_fusion.7 = bf16[16,64,2048]{2,1,0:T(8,128)(2,1)} fusion(bf16[4,64,2048]{2,1,0:T(8,128)(2,1)S(1)} %all-to-all-done.4, s32[1024]{0:T(1024)S(1)} %pad_clamp_fusion), kind=kCustom, calls=%fused_computation.1.clone | custom fusion | bytes 8388672 | tf_op jit(solution)/shard_map/jit(_take)/gather | solution.py:122
  106.1 4.0 %gather_fusion.9 = bf16[16,64,2048]{2,1,0:T(8,128)(2,1)} fusion(bf16[4,64,2048]{2,1,0:T(8,128)(2,1)} %all-to-all-done.5, s32[1024]{0:T(1024)S(1)} %pad_clamp_fusion), kind=kCustom, calls=%fused_computation.3.clone | custom fusion | bytes 8388672 | tf_op jit(solution)/shard_map/jit(_take)/gather | solution.py:123
  110.1 3.5 %fusion.20 = f32[16,2,64]{2,1,0:T(2,128)S(1)} fusion(bf16[16,2,2048]{2,1,0:T(2,128)(2,1)S(1)} %copy-done.9, bf16[16,64,2048]{2,1,0:T(8,128)(2,1)} %gather_fusion.7, pred[16]{0:T(512)(128)(4,1)S(1)} %get-tuple-element.16), kind=kOutput, calls=%fused_computation.35 | convolution fusion | flops 10485760 | bytes 4333584 | tf_op jit(solution)/shard_map/rsd,rkd->rsk/dot_general | solution.py:124
  113.6 10.2 %psum.7 = bf16[16,2,64]{2,1,0:T(2,128)(2,1)S(1)} all-reduce(f32[16,2,64]{2,1,0:T(2,128)S(1)} %fusion.20), channel_id=1, replica_groups=mesh['rep'=2,'req'=4,'mp'=4] {'mp'}, use_global_device_ids=true, to_apply=%region_6.9 | all-reduce | flops 2048 | bytes 12288 | tf_op jit(solution)/shard_map/psum | solution.py:54
  123.8 2.9 %fusion.9 = bf16[16,2,2048]{2,1,0:T(2,128)(2,1)S(1)} fusion(bf16[16,64,2048]{2,1,0:T(8,128)(2,1)} %gather_fusion.9, pred[16]{0:T(512)(128)(4,1)S(1)} %get-tuple-element.16, bf16[16,2,2048]{2,1,0:T(2,128)(2,1)S(1)} %copy-done.10, bf16[16,2,64]{2,1,0:T(2,128)(2,1)S(1)} %psum.7), kind=kOutput, calls=%fused_computation.18 | convolution fusion | flops 10682368 | bytes 4460560 | tf_op jit(solution)/shard_map/gxj,gjv->gxv/dot_general | solution.py:128
  126.9 0.9 fusion.42
  127.8 6.8 %all-to-all-done.1 = bf16[4,2,1,3,128,256]{5,4,3,1,2,0:T(8,128)(2,1)} async-done(((bf16[4,2,1,3,128,256]{5,4,3,1,2,0:T(8,128)(2,1)}), bf16[4,2,1,3,128,256]{5,4,3,1,2,0:T(8,128)(2,1)}, u32[]{:S(2)}, u32[]{:S(2)}) %all-to-all-start.1) | async-done | bytes 1572896 | tf_op jit(solution)/shard_map/all_to_all | solution.py:137
  134.6 1.7 %copy.117 = bf16[2,4,1,3,128,256]{5,4,3,1,0,2:T(8,128)(2,1)S(1)} copy(bf16[2,4,1,3,128,256]{5,4,3,0,2,1:T(8,128)(2,1)} %bitcast.10) | data formatting | bytes 3145728 | tf_op jit(solution)/shard_map/reshape | solution.py:136
  136.3 0.4 copy-done.2
  136.7 2.1 %pad_maximum_fusion = bf16[2,28,128,256]{3,2,1,0:T(8,128)(2,1)} fusion(bf16[2,12,128,256]{3,2,1,0:T(8,128)(2,1)S(1)} %bitcast.62, bf16[2,16,128,256]{3,2,1,0:T(8,128)(2,1)S(1)} %copy-done.2), kind=kLoop, calls=%fused_computation.16 | loop fusion | flops 1835008 | bytes 7340032 | tf_op jit(solution)/shard_map/concatenate | solution.py:140
  138.8 4.2 %gather_fusion.2 = bf16[16,2,128,256]{3,2,1,0:T(8,128)(2,1)} fusion(bf16[2,28,128,256]{3,2,1,0:T(8,128)(2,1)} %pad_maximum_fusion, s32[1024]{0:T(1024)} %pad_clamp_fusion.4), kind=kCustom, calls=%fused_computation.6 | custom fusion | bytes 4194368 | tf_op jit(solution)/shard_map/jit(_take)/gather | solution.py:144
  143.0 1.9 %select_bitcast_fusion = bf16[2,16,128,256]{3,2,0,1:T(8,128)(2,1)S(1)} fusion(bf16[16,2,128,256]{3,2,1,0:T(8,128)(2,1)} %gather_fusion.2, pred[16]{0:T(512)(128)(4,1)S(1)} %copy-done.8), kind=kLoop, calls=%fused_computation.22 | loop fusion | flops 1048576 | bytes 4194320 | tf_op jit(solution)/shard_map/jit(_take)/select_n | solution.py:144
  144.8 1.5 fusion.40
  146.3 1.5 copy.134
  147.8 1.6 %copy.120 = bf16[1,16,128,256]{2,3,1,0:T(8,128)(2,1)S(1)} copy(bf16[1,16,128,256]{3,2,0,1:T(8,128)(2,1)} %get-tuple-element.23) | data formatting | bytes 2097152 | tf_op jit(solution)/shard_map/slice | solution.py:145
  149.4 1.2 fusion.41
  150.6 0.8 reduce_max.32
  151.4 0.3 fusion.24
  151.7 0.9 divide_convert_fusion
  152.6 1.7 %copy.118 = bf16[1,16,128,256]{2,3,1,0:T(8,128)(2,1)S(1)} copy(bf16[1,16,128,256]{3,2,0,1:T(8,128)(2,1)} %get-tuple-element.24) | data formatting | bytes 2097152 | tf_op jit(solution)/shard_map/slice | solution.py:145
  154.3 0.6 convolution_bitcast_fusion.1
  154.9 0.2 fusion.19
  155.1 0.7 reshape.372
  (58 shorter events, 1.7 us)
Async XLA Ops:
  0.6 67.9 %copy-start = (bf16[2,128,16,256]{3,2,1,0:T(8,128)(2,1)S(1)}, bf16[2,128,16,256]{3,2,1,0:T(8,128)(2,1)}, u32[]{:S(2)}) copy-start(bf16[2,128,16,256]{3,2,1,0:T(8,128)(2,1)} %param.22) | copy-start | bytes 6291460
  4.2 12.9 %all-to-all-start.3 = ((s32[4,1,1]{2,1,0:T(1,128)}), s32[4,1,1]{2,1,0:T(1,128)S(1)}, u32[]{:S(2)}, u32[]{:S(2)}) async-start(s32[4,1,1]{2,1,0:T(1,128)} %copy.121), calls=%async_computation.3 | async-start | bytes 4096 | tf_op jit(solution)/shard_map/all_to_all | solution.py:99
  17.1 10.6 %all-to-all-start = ((s32[4,1,3]{2,1,0:T(1,128)}), s32[4,1,3]{2,1,0:T(1,128)S(1)}, u32[]{:S(2)}, u32[]{:S(2)}) async-start(s32[4,1,3]{2,1,0:T(1,128)} %bitcast), calls=%async_computation | async-start | bytes 4096 | tf_op jit(solution)/shard_map/all_to_all | solution.py:100
  27.6 9.5 %all-to-all-start.2 = ((s32[4,1,3]{2,1,0:T(1,128)}), s32[4,1,3]{2,1,0:T(1,128)S(1)}, u32[]{:S(2)}, u32[]{:S(2)}) async-start(s32[4,1,3]{2,1,0:T(1,128)} %bitcast.15), calls=%async_computation.2 | async-start | bytes 4096 | tf_op jit(solution)/shard_map/all_to_all | solution.py:103
  34.6 6.1 %copy-start.5 = (s32[16,8]{0,1:T(8,128)S(1)}, s32[16,8]{0,1:T(8,128)}, u32[]{:S(2)}) copy-start(s32[16,8]{0,1:T(8,128)} %param.23) | copy-start | bytes 1540
  37.1 27.1 %all-to-all-start.4 = ((bf16[4,64,2048]{2,1,0:T(8,128)(2,1)}), bf16[4,64,2048]{2,1,0:T(8,128)(2,1)S(1)}, u32[]{:S(2)}, u32[]{:S(2)}) async-start(bf16[4,64,2048]{2,1,0:T(8,128)(2,1)} %get-tuple-element.29), calls=%async_computation.4 | async-start | bytes 2097152 | tf_op jit(solution)/shard_map/all_to_all | solution.py:115
  64.2 29.5 %all-to-all-start.5 = ((bf16[4,64,2048]{2,1,0:T(8,128)(2,1)}), bf16[4,64,2048]{2,1,0:T(8,128)(2,1)}, u32[]{:S(2)}, u32[]{:S(2)}) async-start(bf16[4,64,2048]{2,1,0:T(8,128)(2,1)} %get-tuple-element.30), calls=%async_computation.5 | async-start | bytes 2097152 | tf_op jit(solution)/shard_map/all_to_all | solution.py:118
  76.7 3.5 %copy-start.4 = (bf16[16,2,2,256]{3,2,1,0:T(2,128)(2,1)S(1)}, bf16[16,2,2,256]{3,2,1,0:T(2,128)(2,1)}, u32[]{:S(2)}) copy-start(bf16[16,2,2,256]{3,2,1,0:T(2,128)(2,1)} %param.17) | copy-start | bytes 98308
  84.2 17.2 %copy-start.7 = (s32[16]{0:T(128)S(1)}, s32[16]{0:T(128)}, u32[]{:S(2)}) copy-start(s32[16]{0:T(128)} %param.25) | copy-start | bytes 196
  84.2 18.4 %copy-start.1 = (s32[16]{0:T(128)S(1)}, s32[16]{0:T(128)}, u32[]{:S(2)}) copy-start(s32[16]{0:T(128)} %param.24) | copy-start | bytes 196
  93.8 40.9 %all-to-all-start.1 = ((bf16[4,2,1,3,128,256]{5,4,3,1,2,0:T(8,128)(2,1)}), bf16[4,2,1,3,128,256]{5,4,3,1,2,0:T(8,128)(2,1)}, u32[]{:S(2)}, u32[]{:S(2)}) async-start(bf16[4,2,1,3,128,256]{5,4,3,1,2,0:T(8,128)(2,1)} %pad_maximum_fusion.1), calls=%async_computation.1 | async-start | bytes 3145728 | tf_op jit(solution)/shard_map/all_to_all | solution.py:137
  106.1 4.0 %copy-start.9 = (bf16[16,2,2048]{2,1,0:T(2,128)(2,1)S(1)}, bf16[16,2,2048]{2,1,0:T(2,128)(2,1)}, u32[]{:S(2)}) copy-start(bf16[16,2,2048]{2,1,0:T(2,128)(2,1)} %param.15) | copy-start | bytes 393220
  110.1 13.7 %copy-start.10 = (bf16[16,2,2048]{2,1,0:T(2,128)(2,1)S(1)}, bf16[16,2,2048]{2,1,0:T(2,128)(2,1)}, u32[]{:S(2)}) copy-start(bf16[16,2,2048]{2,1,0:T(2,128)(2,1)} %param.16) | copy-start | bytes 393220
  123.8 3.1 %copy-start.6 = (bf16[16,2,2,128]{3,2,1,0:T(2,128)(2,1)S(1)}, bf16[16,2,2,128]{3,2,1,0:T(2,128)(2,1)}, u32[]{:S(2)}) copy-start(bf16[16,2,2,128]{3,2,1,0:T(2,128)(2,1)} %reshape.370) | copy-start | bytes 49156
  123.8 3.1 %copy-start.11 = (pred[2,2]{1,0:T(4,128)(4,1)S(1)}, pred[2,2]{1,0:T(4,128)(4,1)}, u32[]{:S(2)}) copy-start(pred[2,2]{1,0:T(4,128)(4,1)} %iota_compare_fusion.5) | copy-start | bytes 16
  134.6 2.1 %copy-start.2 = (bf16[2,16,128,256]{3,2,1,0:T(8,128)(2,1)S(1)}, bf16[2,16,128,256]{3,2,1,0:T(8,128)(2,1)}, u32[]{:S(2)}) copy-start(bf16[2,16,128,256]{3,2,1,0:T(8,128)(2,1)} %bitcast_select_fusion) | copy-start | bytes 6291460
  138.8 4.2 %copy-start.8 = (pred[16]{0:T(512)(128)(4,1)S(1)}, pred[16]{0:T(512)(128)(4,1)}, u32[]{:S(2)}) copy-start(pred[16]{0:T(512)(128)(4,1)} %get-tuple-element.19) | copy-start | bytes 52
  152.6 1.7 %copy-start.3 = (bf16[16,2,2,8,130]{4,3,1,2,0:T(8,128)(2,1)S(1)}, bf16[16,2,2,8,130]{4,3,1,2,0:T(8,128)(2,1)}, u32[]{:S(2)}) copy-start(bf16[16,2,2,8,130]{4,3,1,2,0:T(8,128)(2,1)} %divide_convert_fusion) | copy-start | bytes 399364
